TPU v7x, 32 devices: a whole 2x2x4 slice. The times are simulated.
32 devices in a mesh: group: 2 (over y), chan: 8 (over z, x), rec: 2 (over core).
Axes of the slice: x: 2, y: 2, z: 4, core: 2. Of those that a mesh axis runs over, the one named last changes fastest.
Arguments:
- records: bfloat16 [256, 128, 1024], P(('group', 'chan'), 'rec'), parts along dimension 0, may hold values from -50 to 50
- valid: int32 [256, 128], P(('group', 'chan'), 'rec'), parts along dimension 0, may hold values 0 or 1
- sources: int32 [16], P('group'), parts along dimension 0, may hold values from 0 to 127, as said below
Outputs:
- cross: float32 [256, 8, 1024], P(('group', 'chan'), None, 'rec'), parts along dimension 0
There are 2 independent parts, one for each index of `group`. A program takes and returns all parts, laid end to end along the dimension named above; each array names one. Nothing has to cross between parts.
Inputs may be any that keep to these rules, and one draw needn't show every extreme that they name: `sources`: 8 distinct channel numbers.
All inputs are finite; a program needn't handle non-finite values. No bound on the sum of `valid` on one device may be relied on, other than what follows from the above.
Results may differ from a plain program's by a relative error of at most 0.0034.
Values may be sent and summed in bfloat16 or wider, within the bound.
No kernel may reach another device: no remote copies, remote signals or barrier semaphores. Data moves between devices by JAX's collectives and lax.ppermute only.
A program may use at most 64 MiB of HBM per device.

v0:
```python
import math

import jax
import jax.numpy as jnp
from jax import lax
from jax.sharding import PartitionSpec as P


def dft_table(length, bins):
    times = jnp.arange(length, dtype=jnp.int32)[:, None]
    freqs = jnp.arange(bins, dtype=jnp.int32)[None, :]
    phase = (times * freqs % length).astype(jnp.float32) * (2.0 * math.pi / length)
    return jnp.concatenate([jnp.cos(phase), -jnp.sin(phase)], axis=1).astype(jnp.bfloat16)


def transform(rows, table):
    lead = rows.shape[:-1]
    flat = rows.reshape(-1, rows.shape[-1])
    return jnp.dot(flat, table, preferred_element_type=jnp.float32).reshape(
        lead + (table.shape[1],)
    )


def whiten(spec, bins):
    real_part = spec[..., :bins]
    imag_part = spec[..., bins:]
    power = jnp.mean(real_part * real_part + imag_part * imag_part, axis=-1, keepdims=True)
    return (spec * lax.rsqrt(power + 1e-06)).astype(jnp.bfloat16)


def spread(picked):
    return lax.psum(picked.astype(jnp.float32), "chan").astype(jnp.bfloat16)


def per_device(records, valid, sources):
    per_dev, rec_rows, length = records.shape
    bins = length // 2
    table = dft_table(length, bins)
    masked = records * valid[:, :, None].astype(jnp.bfloat16)
    first = lax.axis_index("chan") * per_dev
    owned = sources[:, None] == first + jnp.arange(per_dev, dtype=jnp.int32)[None, :]
    picked = jnp.einsum(
        "sc,crl->srl", owned.astype(jnp.bfloat16), masked, preferred_element_type=jnp.float32
    ).astype(jnp.bfloat16)
    arrived = spread(picked)
    spectra = transform(masked, table)
    wsrc = whiten(transform(arrived, table), bins)
    hp = lax.Precision.HIGHEST
    xr = spectra[..., :bins]
    xi = spectra[..., bins:]
    wr = wsrc[..., :bins].astype(jnp.float32)
    wi = wsrc[..., bins:].astype(jnp.float32)
    real_sum = jnp.einsum("crf,srf->csf", xr, wr, precision=hp) + jnp.einsum(
        "crf,srf->csf", xi, wi, precision=hp
    )
    imag_sum = jnp.einsum("crf,srf->csf", xi, wr, precision=hp) - jnp.einsum(
        "crf,srf->csf", xr, wi, precision=hp
    )
    partial_stack = jnp.concatenate([real_sum, imag_sum], axis=-1)
    total = lax.psum_scatter(partial_stack, "rec", scatter_dimension=2, tiled=True)
    return total / (rec_rows * lax.axis_size("rec"))


def solution(mesh):
    placed = (P(("group", "chan"), "rec", None), P(("group", "chan"), "rec"), P("group"))
    return jax.shard_map(
        per_device,
        mesh=mesh,
        in_specs=placed,
        out_specs=P(("group", "chan"), None, "rec"),
        check_vma=False,
    )
```

profile of v0, /device:TPU:0, one launch (start us, length us, event | category | flops | bytes accessed | tf_op | source)
XLA Modules:
  0.0 171.4 jit_solution(13488486058295633462)
XLA Ops:
  6.5 0.0 reduce-scatter.2.cloned.1.call-start
  6.5 9.3 %negate_convert_fusion = (bf16[1024,512]{1,0:T(8,128)(2,1)}, bf16[1024,512]{1,0:T(8,128)(2,1)}) fusion(), kind=kLoop, calls=%fused_computation.13 | loop fusion | flops 8912896 | bytes 2097152 | tf_op jit(solution)/shard_map/convert.1
  15.8 0.0 copy-done.4
  15.8 0.0 copy-start.5
  15.9 1.8 %broadcast_multiply_fusion = bf16[16,64,1024]{2,1,0:T(8,128)(2,1)S(1)} fusion(bf16[16,64,1024]{2,1,0:T(8,128)(2,1)} %param.3, bf16[16,64]{1,0:T(8,128)(2,1)S(1)} %convert_element_type.25), kind=kLoop, calls=%fused_computation.26 | loop fusion | flops 1048576 | bytes 4196352 | tf_op jit(solution)/shard_map/mul | solution.py:39
  17.7 0.0 copy-done.5
  17.7 1.3 fusion.3
  18.9 2.0 %fusion.10 = f32[8,64,1024]{2,1,0:T(8,128)} fusion(bf16[8,64,1024]{2,0,1:T(8,128)(2,1)S(1)} %fusion.3), kind=kLoop, calls=%fused_computation.20 | loop fusion | flops 524288 | bytes 3145728 | tf_op jit(solution)/shard_map/convert_element_type | solution.py:32
  20.9 94.7 %all-reduce.1 = bf16[8,64,1024]{2,1,0:T(8,128)(2,1)S(1)} all-reduce(f32[8,64,1024]{2,1,0:T(8,128)} %fusion.10), channel_id=1, replica_groups=mesh['group'=2,'chan'=8,'rec'=2] {'chan'}, use_global_device_ids=true, to_apply=%region_0.1 | all-reduce | flops 524288 | bytes 3145728 | tf_op jit(solution)/shard_map/psum | solution.py:32
  115.6 0.0 copy-start.2
  115.6 4.0 %fusion.8 = f32[16,64,1024]{2,1,0:T(8,128)S(1)} fusion(bf16[16,64,1024]{2,1,0:T(8,128)(2,1)S(1)} %broadcast_multiply_fusion, bf16[1024,512]{1,0:T(8,128)(2,1)} %get-tuple-element.9, bf16[1024,512]{1,0:T(8,128)(2,1)} %get-tuple-element.10), kind=kOutput, calls=%fused_computation.18 | convolution fusion | flops 2151677952 | bytes 8388608 | tf_op jit(solution)/shard_map/dot_general | solution.py:19
  119.7 0.0 copy-done.2
  119.7 0.0 copy-done.3
  119.7 1.2 fusion.9
  120.9 2.7 %fusion.20 = (f32[16,64,512]{2,1,0:T(8,128)}, f32[16,64,512]{2,1,0:T(8,128)}) fusion(f32[16,64,1024]{2,1,0:T(8,128)S(1)} %fusion.8), kind=kLoop, calls=%fused_computation.37 | loop fusion | bytes 8388608 | tf_op jit(solution)/shard_map/slice | solution.py:49
  123.7 0.2 fusion.12
  123.9 0.2 multiply_convert_fusion
  124.1 0.1 fusion.21
  124.2 0.8 copy.15
  124.9 0.8 copy.13
  125.7 4.8 %copy.14 = f32[16,64,512]{1,0,2:T(8,128)} copy(f32[16,64,512]{2,1,0:T(8,128)} %get-tuple-element.5) | data formatting | bytes 4194304 | tf_op jit(solution)/shard_map/slice | solution.py:49
  130.6 4.9 %copy.16 = f32[16,64,512]{1,0,2:T(8,128)} copy(f32[16,64,512]{2,1,0:T(8,128)} %get-tuple-element.6) | data formatting | bytes 4194304 | tf_op jit(solution)/shard_map/slice | solution.py:50
  135.5 5.4 %fusion.22 = f32[512,8,16]{2,1,0:T(8,128)S(1)} fusion(bf16[8,64,512]{1,0,2:T(8,128)(2,1)S(1)} %copy.13, f32[16,64,512]{1,0,2:T(8,128)} %copy.14), kind=kOutput, calls=%fused_computation.39 | convolution fusion | flops 50331648 | bytes 2883584 | tf_op jit(solution)/shard_map/crf,srf->csf/dot_general | solution.py:53
  140.9 3.4 %fusion.23 = f32[512,8,16]{2,1,0:T(8,128)S(1)} fusion(bf16[8,64,512]{1,0,2:T(8,128)(2,1)S(1)} %copy.13, f32[16,64,512]{1,0,2:T(8,128)S(1)} %copy-done.1), kind=kOutput, calls=%fused_computation.40 | convolution fusion | flops 50331648 | bytes 2883584 | tf_op jit(solution)/shard_map/crf,srf->csf/dot_general | solution.py:56
  144.3 3.4 %add_bitcast_fusion = f32[16,8,512]{0,1,2:T(8,128)S(1)} fusion(f32[512,8,16]{2,1,0:T(8,128)S(1)} %fusion.22, bf16[8,64,512]{1,0,2:T(8,128)(2,1)S(1)} %copy.15, f32[16,64,512]{1,0,2:T(8,128)S(1)} %copy-done.1), kind=kOutput, calls=%fused_computation.11 | convolution fusion | flops 50397184 | bytes 3145728 | tf_op jit(solution)/shard_map/crf,srf->csf/dot_general | solution.py:53
  147.7 4.7 %subtract_bitcast_fusion = f32[16,8,512]{0,1,2:T(8,128)} fusion(f32[512,8,16]{2,1,0:T(8,128)S(1)} %fusion.23, bf16[8,64,512]{1,0,2:T(8,128)(2,1)S(1)} %copy.15, f32[16,64,512]{1,0,2:T(8,128)S(1)} %copy-done), kind=kOutput, calls=%fused_computation.10 | convolution fusion | flops 50397184 | bytes 3145728 | tf_op jit(solution)/shard_map/crf,srf->csf/dot_general | solution.py:56
  152.4 2.3 %copy.22 = f32[16,8,512]{2,1,0:T(8,128)S(1)} copy(f32[16,8,512]{0,1,2:T(8,128)} %subtract_bitcast_fusion) | data formatting | bytes 524288 | tf_op jit(solution)/shard_map/sub | solution.py:56
  154.7 0.8 copy.21
  155.4 0.8 pad_maximum_fusion
  156.3 0.0 reduce-scatter.2.cloned.1.call-update
  156.3 6.6 %reduce-scatter.2.cloned.1.call-done = f32[16,8,512]{2,1,0:T(8,128)} async-done(((f32[16,8,1024]{2,1,0:T(8,128)}), f32[16,8,512]{2,1,0:T(8,128)}) %reduce-scatter.2.cloned.1.call-update) | async-done | bytes 262160 | tf_op jit(solution)/shard_map/reduce_scatter | solution.py:60
  162.8 1.7 broadcast_multiply_fusion.1
  (9 shorter events, 0.0 us)
Async XLA Ops:
  6.5 9.3 %copy-start.4 = (s32[16,64]{1,0:T(8,128)S(1)}, s32[16,64]{1,0:T(8,128)}, u32[]{:S(2)}) copy-start(s32[16,64]{1,0:T(8,128)} %param.4) | copy-start | bytes 12292
  6.5 156.3 %reduce-scatter.2.cloned.1.call-start = ((), (), s32[]{:S(2)}) async-start(), calls=%async_computation.1 | async-start | bytes 786432 | tf_op jit(solution)/shard_map/reduce_scatter | solution.py:60
  15.8 1.8 %copy-start.5 = (s32[8]{0:T(128)S(1)}, s32[8]{0:T(128)}, u32[]{:S(2)}) copy-start(s32[8]{0:T(128)} %param.5) | copy-start | bytes 100
  115.6 4.0 %copy-start.2 = (bf16[1024,512]{1,0:T(8,128)(2,1)S(1)}, bf16[1024,512]{1,0:T(8,128)(2,1)}, u32[]{:S(2)}) copy-start(bf16[1024,512]{1,0:T(8,128)(2,1)} %get-tuple-element.9) | copy-start | bytes 3145732
  115.6 4.0 %copy-start.3 = (bf16[1024,512]{1,0:T(8,128)(2,1)S(1)}, bf16[1024,512]{1,0:T(8,128)(2,1)}, u32[]{:S(2)}) copy-start(bf16[1024,512]{1,0:T(8,128)(2,1)} %get-tuple-element.10) | copy-start | bytes 3145732
  135.5 5.5 %copy-start.1 = (f32[16,64,512]{1,0,2:T(8,128)S(1)}, f32[16,64,512]{1,0,2:T(8,128)}, u32[]{:S(2)}) copy-start(f32[16,64,512]{1,0,2:T(8,128)} %copy.16) | copy-start | bytes 6291460
  144.3 3.4 %copy-start = (f32[16,64,512]{1,0,2:T(8,128)S(1)}, f32[16,64,512]{1,0,2:T(8,128)}, u32[]{:S(2)}) copy-start(f32[16,64,512]{1,0,2:T(8,128)} %copy.14) | copy-start | bytes 6291460
Sparse Core Ops, SparseCore 0:
  156.4 6.3 reduce-scatter.1
where the time goes:
time: 172 us; the launch traced here: 171 us
  blocking collectives  94.7 us (55%)
  matrix products  23.4 us (14%)
  local copies, waits for them, and re-layouts  17.1 us (10%)
  other arithmetic  15.9 us (9%)
  between operations  13.6 us (8%)
  waiting for transfers between devices  6.58 us (4%)
    psum x1, blocking collectives, spread(): return lax.psum(picked.astype(jnp.float32), 'chan').astype(jnp.bfloat16)  94.7 us
    another operation x1, other arithmetic  9.29 us
    slice x2, local copies, waits for them, and re-layouts, per_device(): xr = spectra[..., :bins]  7.57 us
    reduce_scatter x1, waiting for transfers between devices, per_device(): lax.psum_scatter(partial_stack, 'rec', scatter_dimension=2, tiled=True)  6.57 us
    dot_general x1, matrix products, per_device(): jnp.einsum('crf,srf->csf', xr, wr, precision=hp)  5.44 us
    dot_general x2, matrix products, transform(): jnp.dot(flat, table, preferred_element_type=jnp.float32)  5.26 us
    slice x1, local copies, waits for them, and re-layouts, per_device(): xi = spectra[..., bins:]  4.88 us
    dot_general x1, matrix products, per_device(): jnp.einsum('crf,srf->csf', xr, wi, precision=hp)  4.71 us
  transfers between devices with their start and end apart: 1, of which 1 were waited for; matrix products, arithmetic and copies ran while one was open for 0% of the time, Pallas kernels for 0%

commit v1 on v0

v1 whole, which is shorter than its diff:
```python
import functools
import math

import jax
import jax.numpy as jnp
import numpy as np
from jax import lax
from jax.experimental import pallas as pl
from jax.experimental.pallas import tpu as pltpu
from jax.sharding import PartitionSpec as P

VMEM = pl.BlockSpec(memory_space=pltpu.VMEM)
SMEM = pl.BlockSpec(memory_space=pltpu.SMEM)
LANES = 128
QUAD = 4
ROOM = pltpu.CompilerParams(vmem_limit_bytes=16 << 20)


def dft_table(length, bins):
    times = np.arange(length)[:, None]
    freqs = np.arange(bins)[None, :]
    phase = (times * freqs % length) * (2.0 * math.pi / length)
    table = np.concatenate([np.cos(phase), -np.sin(phase)], axis=1)
    return jnp.asarray(table.astype(np.float32).astype(jnp.bfloat16))


def row_mask(valid_row, start, rows):
    n = valid_row.shape[1]
    lane = lax.broadcasted_iota(jnp.int32, (rows, n), 1)
    row = lax.broadcasted_iota(jnp.int32, (rows, n), 0)
    hit = jnp.where(lane == row + start, valid_row.astype(jnp.float32), 0.0)
    return jnp.sum(hit, axis=1, keepdims=True)


def pick_kernel(sources, valid, records, *outs):
    per_dev, rec_rows, _ = records.shape
    block = rec_rows // QUAD
    me = lax.axis_index("chan")
    quad = lax.rem(me, QUAD)
    for s in range(sources.shape[0]):
        local = sources[s] - me * per_dev
        owned = jnp.logical_and(local >= 0, local < per_dev)

        @pl.when(owned)
        def _():
            row = valid[pl.ds(local, 1), :]
            for j, out in enumerate(outs):
                start = pl.multiple_of((quad ^ j) * block, block)
                part = records[local, pl.ds(start, block), :].astype(jnp.float32)
                out[s] = (part * row_mask(row, start, block)).astype(out.dtype)

        @pl.when(jnp.logical_not(owned))
        def _():
            for out in outs:
                out[s] = jnp.zeros(out.shape[1:], out.dtype)


def pick(sources, valid, records):
    n_src = sources.shape[0]
    _, rec_rows, length = records.shape
    part = jax.ShapeDtypeStruct((n_src, rec_rows // QUAD, length), records.dtype)
    return pl.pallas_call(
        pick_kernel,
        out_shape=(part,) * QUAD,
        in_specs=[SMEM, VMEM, VMEM],
        out_specs=(VMEM,) * QUAD,
        compiler_params=ROOM,
        name="pick",
    )(sources, valid, records)


def spectra_kernel(valid, table, records, out):
    chans, rec_rows, length = records.shape
    step = pl.program_id(0)
    flat = records[...].reshape(chans * rec_rows, length)
    spec = jnp.dot(flat, table[...], preferred_element_type=jnp.float32)
    for c in range(chans):
        mask = row_mask(valid[pl.ds(step * chans + c, 1), :], 0, rec_rows)
        part = spec[c * rec_rows : (c + 1) * rec_rows] * mask
        for f in range(out.shape[0]):
            out[f, c] = part[:, f * LANES : (f + 1) * LANES]


def spectra_of(valid, table, records, chans=2):
    per_dev, rec_rows, length = records.shape
    width = table.shape[1]
    return pl.pallas_call(
        spectra_kernel,
        out_shape=jax.ShapeDtypeStruct((width // LANES, per_dev, rec_rows, LANES), jnp.float32),
        grid=(per_dev // chans,),
        in_specs=[
            VMEM,
            VMEM,
            pl.BlockSpec((chans, rec_rows, length), lambda i: (i, 0, 0)),
        ],
        out_specs=pl.BlockSpec(
            (width // LANES, chans, rec_rows, LANES), lambda i: (0, i, 0, 0)
        ),
        cost_estimate=pl.CostEstimate(
            flops=2 * per_dev * rec_rows * length * width,
            bytes_accessed=per_dev * rec_rows * (2 * length + 4 * width),
            transcendentals=0,
        ),
        compiler_params=ROOM,
        name="spectra",
    )(valid, table, records)


def whiten_kernel(table, mine, other, out, mixed):
    n_src, block, length = mine.shape
    bins = table.shape[1] // 2
    rows = (mine[...] + other[...]).reshape(n_src * block, length)
    spec = jnp.dot(rows, table[...], preferred_element_type=jnp.float32)
    real, imag = spec[:, :bins], spec[:, bins:]
    power = jnp.sum(real * real + imag * imag, axis=1, keepdims=True) / bins
    white = spec * lax.rsqrt(power + 1e-06)
    for f in range(0, 2 * bins, LANES):
        for s in range(n_src):
            part = white[s * block : (s + 1) * block, f : f + LANES]
            mixed[f // LANES, pl.ds(s, block, stride=n_src), :] = part
        out[:, f : f + LANES] = mixed[f // LANES].astype(out.dtype)


def whitened_of(table, mine, other):
    n_src, block, _ = mine.shape
    width = table.shape[1]
    rows = n_src * block
    return pl.pallas_call(
        whiten_kernel,
        out_shape=jax.ShapeDtypeStruct((rows, width), jnp.bfloat16),
        in_specs=[VMEM, VMEM, VMEM],
        out_specs=VMEM,
        scratch_shapes=[pltpu.VMEM((width // LANES, rows, LANES), jnp.float32)],
        compiler_params=ROOM,
        name="whiten",
    )(table, mine, other)


def cross_kernel(other, mode, first, spectra, white, *rest):
    both = mode == "both"
    acc, out, conj = (None, *rest) if first else rest
    chans = spectra.shape[1]
    rows, width = white.shape
    n_src = out.shape[-2]
    block = rows // n_src
    bins = width // 2
    quad = lax.rem(lax.axis_index("chan"), QUAD)
    base = (quad ^ other) * block
    core = lax.axis_index("rec")
    part = core if mode == "keep" else 1 - core
    tiles = bins // LANES
    for f in range(tiles):
        real = white[:, f * LANES : (f + 1) * LANES].astype(jnp.float32)
        imag = white[:, bins + f * LANES : bins + (f + 1) * LANES].astype(jnp.float32)
        conj[0, f] = real if both else jnp.where(part == 0, real, -imag)
        conj[1, f] = imag if both else jnp.where(part == 0, imag, real)
    group = 8 if both else chans

    @pl.loop(0, tiles)
    def _(f):
        lo = pl.multiple_of(f * LANES, LANES)
        for c0 in range(0, chans, group):
            names = range(c0, c0 + group)
            if both:
                spots_of = [(p, c) for c in names for p in (0, 1)]
            else:
                spots_of = [(part, c) for c in names]
            if first:
                sums = [jnp.zeros((n_src, LANES), jnp.float32) for _ in spots_of]
            else:
                sums = [acc[p, c, :, pl.ds(lo, LANES)] for p, c in spots_of]

            def add(r, sums):
                a = conj[0, f, pl.ds(r * n_src, n_src), :]
                b = conj[1, f, pl.ds(r * n_src, n_src), :]
                new = []
                for i, c in enumerate(names):
                    xr = spectra[f, c, pl.ds(base + r, 1), :]
                    xi = spectra[tiles + f, c, pl.ds(base + r, 1), :]
                    if both:
                        new.append(sums[2 * i] + (xr * a + xi * b))
                        new.append(sums[2 * i + 1] + (xi * a - xr * b))
                    else:
                        new.append(sums[i] + (xr * a + xi * b))
                return new

            for r in range(block):
                sums = add(r, sums)
            for (p, c), total in zip(spots_of, sums):
                if both:
                    out[p, c, :, pl.ds(lo, LANES)] = total
                else:
                    out[c, :, pl.ds(lo, LANES)] = total


def cross_of(spectra, white, n_src, other, mode, acc=None):
    both = mode == "both"
    chans = spectra.shape[1]
    rows, width = white.shape
    bins = width // 2
    shape = (2, chans, n_src, bins) if both else (chans, n_src, bins)
    args = (spectra, white) + (() if acc is None else (acc,))
    parts = 2 if both else 1
    return pl.pallas_call(
        functools.partial(cross_kernel, other, mode, acc is None),
        out_shape=jax.ShapeDtypeStruct(shape, jnp.float32),
        in_specs=[VMEM] * len(args),
        out_specs=VMEM,
        scratch_shapes=[pltpu.VMEM((2, bins // LANES, rows, LANES), jnp.float32)],
        input_output_aliases={2: 0} if both and acc is not None else {},
        cost_estimate=pl.CostEstimate(
            flops=4 * parts * chans * rows * bins * 16,
            bytes_accessed=rows * chans * width,
            transcendentals=0,
        ),
        compiler_params=ROOM,
        name="cross_" + mode,
    )(*args)


def per_device(records, valid, sources):
    per_dev, rec_rows, length = records.shape
    bins = length // 2
    n_src = sources.shape[0]
    n_chan = lax.axis_size("chan")
    n_rec = lax.axis_size("rec")
    table = dft_table(length, bins)

    def swap(value, bit):
        return lax.ppermute(value, "chan", [(i, i ^ bit) for i in range(n_chan)])

    picked = pick(sources, valid, records)
    arrived = [swap(picked[j], j) for j in (3, 1, 2)]
    spectra = spectra_of(valid, table, records)
    *arrived, spectra = lax.optimization_barrier((*arrived, spectra))
    home = picked[0] + arrived[0] + arrived[1] + arrived[2]
    bit = QUAD
    while bit * 2 < n_chan:
        home = home + swap(home, bit)
        bit *= 2
    white = whitened_of(table, home, swap(home, bit))
    others = [(j, swap(white, j)) for j in (1, 2, 3)]

    acc = cross_of(spectra, white, n_src, 0, "both")
    for j, block in others[:2]:
        acc = cross_of(spectra, block, n_src, j, "both", acc)
    j, block = others[2]
    send = cross_of(spectra, block, n_src, j, "send", acc)
    came = lax.ppermute(send, "rec", [(i, i ^ 1) for i in range(n_rec)])
    keep = cross_of(spectra, block, n_src, j, "keep", acc)
    return (keep + came) / (rec_rows * n_rec)


def solution(mesh):
    placed = (P(("group", "chan"), "rec", None), P(("group", "chan"), "rec"), P("group"))
    return jax.shard_map(
        per_device,
        mesh=mesh,
        in_specs=placed,
        out_specs=P(("group", "chan"), None, "rec"),
        check_vma=False,
    )
```

time: 172 us -> 53.2 us (0.31)
  blocking collectives: 94.7 us -> 0 us
  matrix products: 23.4 us -> 0 us
  waiting for transfers between devices: 6.58 us -> 26.3 us
  other arithmetic: 15.9 us -> 0.81 us
  between operations: 13.6 us -> 0.07 us
  local copies, waits for them, and re-layouts: 17.1 us -> 4.54 us
  starting transfers between devices: 0.01 us -> 10.9 us
  Pallas kernels: 0 us -> 10.5 us
    psum x1 -> x0, blocking collectives: 94.7 us -> none  [spread(): return lax.psum(picked.astype(jnp.float32), 'chan').astype(jnp.bfloat16)]
    ppermute x0 -> x8, waiting for transfers between devices: none -> 26.3 us  [the longest x7 25.5 us: swap(): return lax.ppermute(value, 'chan', [(i, i ^ bit) for i in range(n_chan)])]
    dot_general x7 -> x0, matrix products: 23.4 us -> none  [the longest x1 5.44 us: per_device(): jnp.einsum('crf,srf->csf', xr, wr, precision=hp)]
    slice x6 -> x0, local copies, waits for them, and re-layouts: 14.1 us -> none  [the longest x2 7.57 us: per_device(): xr = spectra[..., :bins]]
    ppermute x0 -> x8, starting transfers between devices: none -> 10.9 us  [the longest x7 10.8 us: swap(): return lax.ppermute(value, 'chan', [(i, i ^ bit) for i in range(n_chan)])]
    pallas_call x0 -> x8, Pallas kernels: none -> 10.5 us  [the longest x5 5.15 us: cross_of(): pl.pallas_call(functools.partial(cross_kernel, other, mode, acc is None),...]
    another operation x1 -> x0, other arithmetic: 9.29 us -> none
    reduce_scatter x1 -> x0, waiting for transfers between devices: 6.57 us -> none  [per_device(): lax.psum_scatter(partial_stack, 'rec', scatter_dimension=2, tiled=True)]
  transfers between devices with their start and end apart: 1 -> 8, of which waited for: 1 -> 8; matrix products, arithmetic and copies ran while one was open for 0% -> 0% of each run, Pallas kernels for 0% -> 16%
where the time goes in v1:
time: 53.2 us; the launch traced here: 53.1 us
  waiting for transfers between devices  26.3 us (49%)
  starting transfers between devices  10.9 us (20%)
  Pallas kernels  10.5 us (20%)
  local copies, waits for them, and re-layouts  4.54 us (9%)
  other arithmetic  0.81 us (2%)
    ppermute x7, waiting for transfers between devices, swap(): return lax.ppermute(value, 'chan', [(i, i ^ bit) for i in range(n_chan)])  25.5 us
    ppermute x7, starting transfers between devices, swap(): return lax.ppermute(value, 'chan', [(i, i ^ bit) for i in range(n_chan)])  10.8 us
    pallas_call x5, Pallas kernels, cross_of(): pl.pallas_call(functools.partial(cross_kernel, other, mode, acc is None),...  5.15 us
    unnamed x12, local copies, waits for them, and re-layouts  4.54 us
    pallas_call x1, Pallas kernels, spectra_of(): pl.pallas_call(spectra_kernel, out_shape=jax.ShapeDtypeStruct((width // L...  3.92 us
  transfers between devices with their start and end apart: 8, of which 8 were waited for; matrix products, arithmetic and copies ran while one was open for 0% of the time, Pallas kernels for 16%

profile of v1, /device:TPU:0, one launch (start us, length us, event | category | flops | bytes accessed | tf_op | source)
XLA Modules:
  0.0 53.1 jit_solution(9917874138467565088)
XLA Ops:
  0.0 1.6 %copy-done = bf16[16,64,1024]{2,1,0:T(8,128)(2,1)S(1)} copy-done((bf16[16,64,1024]{2,1,0:T(8,128)(2,1)S(1)}, bf16[16,64,1024]{2,1,0:T(8,128)(2,1)}, u32[]{:S(2)}) %copy-start) | copy-done | bytes 2097176
  1.6 0.7 %copy-done.4 = s32[16,64]{1,0:T(8,128)S(1)} copy-done((s32[16,64]{1,0:T(8,128)S(1)}, s32[16,64]{1,0:T(8,128)}, u32[]{:S(2)}) %copy-start.4) | copy-done | bytes 4120
  2.3 0.7 %copy-done.5 = s32[8]{0:T(128)S(1)} copy-done((s32[8]{0:T(128)S(1)}, s32[8]{0:T(128)}, u32[]{:S(2)}) %copy-start.5) | copy-done | bytes 56
  2.9 0.8 %pick.1 = (bf16[8,16,1024]{2,1,0:T(8,128)(2,1)S(1)}, bf16[8,16,1024]{2,1,0:T(8,128)(2,1)S(1)}, bf16[8,16,1024]{2,1,0:T(8,128)(2,1)S(1)}, bf16[8,16,1024]{2,1,0:T(8,128)(2,1)S(1)}) custom-call(s32[8]{0:T(128)S(1)} %copy-done.5, s32[16,64]{1,0:T(8,128)S(1)} %copy-done.4, bf16[16,64,1024]{2,1,0:T(8,128)(2,1)S(1)} %copy-done), custom_call_target="tpu_custom_call" | custom-call | tf_op jit(solution)/shard_map/pick/pallas_call | solution.py:62
  3.7 4.0 %collective-permute-start = (bf16[8,16,1024]{2,1,0:T(8,128)(2,1)S(1)}, bf16[8,16,1024]{2,1,0:T(8,128)(2,1)S(1)}, u32[]{:S(2)}, u32[]{:S(2)}) collective-permute-start(bf16[8,16,1024]{2,1,0:T(8,128)(2,1)S(1)} %get-tuple-element.13), channel_id=1, source_target_pairs={{0,6},{2,4},{4,2},{6,0},{8,14},{10,12},{12,10},{14,8},{1,7},{3,5},... | collective-permute-start | bytes 786440 | tf_op jit(solution)/shard_map/ppermute | solution.py:230
  7.7 0.6 %collective-permute-start.1 = (bf16[8,16,1024]{2,1,0:T(8,128)(2,1)S(1)}, bf16[8,16,1024]{2,1,0:T(8,128)(2,1)S(1)}, u32[]{:S(2)}, u32[]{:S(2)}) collective-permute-start(bf16[8,16,1024]{2,1,0:T(8,128)(2,1)S(1)} %get-tuple-element.14), channel_id=1, source_target_pairs={{0,2},{2,0},{4,6},{6,4},{8,10},{10,8},{12,14},{14,12},{1,3},{3,1},... | collective-permute-start | bytes 786440 | tf_op jit(solution)/shard_map/ppermute | solution.py:230
  8.3 0.0 collective-permute-start.2
  8.3 0.0 copy-done.1
  8.3 1.6 %copy-done.2 = bf16[1024,1024]{1,0:T(8,128)(2,1)S(1)} copy-done((bf16[1024,1024]{1,0:T(8,128)(2,1)S(1)}, bf16[1024,1024]{1,0:T(8,128)(2,1)}, u32[]{:S(2)}) %copy-start.2) | copy-done | bytes 2097176
  9.9 3.9 %spectra.1 = f32[8,16,64,128]{3,2,1,0:T(8,128)S(1)} custom-call(s32[16,64]{1,0:T(8,128)S(1)} %copy-done.4, bf16[1024,1024]{1,0:T(8,128)(2,1)S(1)} %copy-done.2, bf16[16,64,1024]{2,1,0:T(8,128)(2,1)S(1)} %copy-done.1), custom_call_target="tpu_custom_call" | custom-call | flops 2147483648 | bytes 6291456 | tf_op jit(solution)/shard_map/spectra/pallas_call | solution.py:87
  13.9 1.0 %collective-permute-done = bf16[8,16,1024]{2,1,0:T(8,128)(2,1)S(1)} collective-permute-done((bf16[8,16,1024]{2,1,0:T(8,128)(2,1)S(1)}, bf16[8,16,1024]{2,1,0:T(8,128)(2,1)S(1)}, u32[]{:S(2)}, u32[]{:S(2)}) %collective-permute-start) | collective-permute-done | bytes 262176 | tf_op jit(solution)/shard_map/ppermute | solution.py:230
  14.9 4.7 %collective-permute-done.1 = bf16[8,16,1024]{2,1,0:T(8,128)(2,1)S(1)} collective-permute-done((bf16[8,16,1024]{2,1,0:T(8,128)(2,1)S(1)}, bf16[8,16,1024]{2,1,0:T(8,128)(2,1)S(1)}, u32[]{:S(2)}, u32[]{:S(2)}) %collective-permute-start.1) | collective-permute-done | bytes 262176 | tf_op jit(solution)/shard_map/ppermute | solution.py:230
  19.6 0.3 collective-permute-done.2
  19.9 0.1 add_add_fusion.mine
  20.0 2.7 %collective-permute-start.3 = (bf16[8,16,1024]{2,1,0:T(8,128)(2,1)S(1)}, bf16[8,16,1024]{2,1,0:T(8,128)(2,1)S(1)}, u32[]{:S(2)}, u32[]{:S(2)}) collective-permute-start(bf16[8,16,1024]{2,1,0:T(8,128)(2,1)S(1)} %add_add_fusion.mine), channel_id=1, source_target_pairs={{0,8},{2,10},{4,12},{6,14},{8,0},{10,2},{12,4},{14,6},{1,9},{3,11}... | collective-permute-start | bytes 786440 | tf_op jit(solution)/shard_map/ppermute | solution.py:230
  22.7 12.1 %collective-permute-done.3.other = bf16[8,16,1024]{2,1,0:T(8,128)(2,1)S(1)} collective-permute-done((bf16[8,16,1024]{2,1,0:T(8,128)(2,1)S(1)}, bf16[8,16,1024]{2,1,0:T(8,128)(2,1)S(1)}, u32[]{:S(2)}, u32[]{:S(2)}) %collective-permute-start.3) | collective-permute-done | bytes 262176 | tf_op jit(solution)/shard_map/ppermute | solution.py:230
  34.8 0.0 copy-done.3
  34.8 0.7 %whiten.1.white = bf16[128,1024]{1,0:T(8,128)(2,1)S(1)} custom-call(bf16[1024,1024]{1,0:T(8,128)(2,1)S(1)} %copy-done.3, bf16[8,16,1024]{2,1,0:T(8,128)(2,1)S(1)} %add_add_fusion.mine, bf16[8,16,1024]{2,1,0:T(8,128)(2,1)S(1)} %collective-permute-done.3.other), custom_call_target="tpu_custom_call" | custom-call | tf_op jit(solution)/shard_map/whiten/pallas_call | solution.py:128
  35.4 1.1 %collective-permute-start.6 = (bf16[128,1024]{1,0:T(8,128)(2,1)S(1)}, bf16[128,1024]{1,0:T(8,128)(2,1)S(1)}, u32[]{:S(2)}, u32[]{:S(2)}) collective-permute-start(bf16[128,1024]{1,0:T(8,128)(2,1)S(1)} %whiten.1.white), channel_id=1, source_target_pairs={{0,2},{2,0},{4,6},{6,4},{8,10},{10,8},{12,14},{14,12},{1,3},{3,1},... | collective-permute-start | bytes 786440 | tf_op jit(solution)/shard_map/ppermute | solution.py:230
  36.6 0.0 collective-permute-start.5
  36.6 2.4 %collective-permute-start.4 = (bf16[128,1024]{1,0:T(8,128)(2,1)S(1)}, bf16[128,1024]{1,0:T(8,128)(2,1)S(1)}, u32[]{:S(2)}, u32[]{:S(2)}) collective-permute-start(bf16[128,1024]{1,0:T(8,128)(2,1)S(1)} %whiten.1.white), channel_id=1, source_target_pairs={{0,6},{2,4},{4,2},{6,0},{8,14},{10,12},{12,10},{14,8},{1,7},{3,5},... | collective-permute-start | bytes 786440 | tf_op jit(solution)/shard_map/ppermute | solution.py:230
  39.0 1.2 %cross_both.3.rest_0_ = f32[2,16,8,512]{3,2,1,0:T(8,128)S(1)} custom-call(f32[8,16,64,128]{3,2,1,0:T(8,128)S(1)} %spectra.1, bf16[128,1024]{1,0:T(8,128)(2,1)S(1)} %whiten.1.white), custom_call_target="tpu_custom_call" | custom-call | flops 134217728 | bytes 2097152 | tf_op jit(solution)/shard_map/cross_both/pallas_call | solution.py:204
  40.2 3.4 %collective-permute-done.6.white = bf16[128,1024]{1,0:T(8,128)(2,1)S(1)} collective-permute-done((bf16[128,1024]{1,0:T(8,128)(2,1)S(1)}, bf16[128,1024]{1,0:T(8,128)(2,1)S(1)}, u32[]{:S(2)}, u32[]{:S(2)}) %collective-permute-start.6) | collective-permute-done | bytes 262176 | tf_op jit(solution)/shard_map/ppermute | solution.py:230
  43.6 1.2 %cross_both.4.rest_0_ = f32[2,16,8,512]{3,2,1,0:T(8,128)S(1)} custom-call(f32[8,16,64,128]{3,2,1,0:T(8,128)S(1)} %spectra.1, bf16[128,1024]{1,0:T(8,128)(2,1)S(1)} %collective-permute-done.6.white, f32[2,16,8,512]{3,2,1,0:T(8,128)S(1)} %cross_both.3.rest_0_), custom_call_target="tpu_custom_call", output_to_operand_aliasing={{}: (2, {})} | custom-call | flops 134217728 | bytes 2097152 | tf_op jit(solution)/shard_map/cross_both/pallas_call | solution.py:204
  44.8 0.9 %collective-permute-done.5.white = bf16[128,1024]{1,0:T(8,128)(2,1)S(1)} collective-permute-done((bf16[128,1024]{1,0:T(8,128)(2,1)S(1)}, bf16[128,1024]{1,0:T(8,128)(2,1)S(1)}, u32[]{:S(2)}, u32[]{:S(2)}) %collective-permute-start.5) | collective-permute-done | bytes 262176 | tf_op jit(solution)/shard_map/ppermute | solution.py:230
  45.8 1.2 %cross_both.5.rest_0_ = f32[2,16,8,512]{3,2,1,0:T(8,128)S(1)} custom-call(f32[8,16,64,128]{3,2,1,0:T(8,128)S(1)} %spectra.1, bf16[128,1024]{1,0:T(8,128)(2,1)S(1)} %collective-permute-done.5.white, f32[2,16,8,512]{3,2,1,0:T(8,128)S(1)} %cross_both.4.rest_0_), custom_call_target="tpu_custom_call", output_to_operand_aliasing={{}: (2, {})} | custom-call | flops 134217728 | bytes 2097152 | tf_op jit(solution)/shard_map/cross_both/pallas_call | solution.py:204
  46.9 3.0 %collective-permute-done.4.white = bf16[128,1024]{1,0:T(8,128)(2,1)S(1)} collective-permute-done((bf16[128,1024]{1,0:T(8,128)(2,1)S(1)}, bf16[128,1024]{1,0:T(8,128)(2,1)S(1)}, u32[]{:S(2)}, u32[]{:S(2)}) %collective-permute-start.4) | collective-permute-done | bytes 262176 | tf_op jit(solution)/shard_map/ppermute | solution.py:230
  50.0 0.8 %cross_send.1 = f32[16,8,512]{2,1,0:T(8,128)S(1)} custom-call(f32[8,16,64,128]{3,2,1,0:T(8,128)S(1)} %spectra.1, bf16[128,1024]{1,0:T(8,128)(2,1)S(1)} %collective-permute-done.4.white, f32[2,16,8,512]{3,2,1,0:T(8,128)S(1)} %cross_both.5.rest_0_), custom_call_target="tpu_custom_call" | custom-call | flops 67108864 | bytes 2097152 | tf_op jit(solution)/shard_map/cross_send/pallas_call | solution.py:204
  50.8 0.1 collective-permute-start.7
  50.8 0.8 %cross_keep.1 = f32[16,8,512]{2,1,0:T(8,128)S(1)} custom-call(f32[8,16,64,128]{3,2,1,0:T(8,128)S(1)} %spectra.1, bf16[128,1024]{1,0:T(8,128)(2,1)S(1)} %collective-permute-done.4.white, f32[2,16,8,512]{3,2,1,0:T(8,128)S(1)} %cross_both.5.rest_0_), custom_call_target="tpu_custom_call" | custom-call | flops 67108864 | bytes 2097152 | tf_op jit(solution)/shard_map/cross_keep/pallas_call | solution.py:204
  51.6 0.7 %collective-permute-done.7 = f32[16,8,512]{2,1,0:T(8,128)S(1)} collective-permute-done((f32[16,8,512]{2,1,0:T(8,128)S(1)}, f32[16,8,512]{2,1,0:T(8,128)S(1)}, u32[]{:S(2)}, u32[]{:S(2)}) %collective-permute-start.7) | collective-permute-done | bytes 262176 | tf_op jit(solution)/shard_map/ppermute | solution.py:249
  52.4 0.7 %add_multiply_fusion = f32[16,8,512]{2,1,0:T(8,128)} fusion(f32[16,8,512]{2,1,0:T(8,128)S(1)} %cross_keep.1, f32[16,8,512]{2,1,0:T(8,128)S(1)} %collective-permute-done.7), kind=kLoop, calls=%fused_computation | loop fusion | flops 131072 | bytes 786432 | tf_op jit(solution)/shard_map/div | solution.py:251
  (6 shorter events, 0.0 us)
Async XLA Ops:
  0.0 1.6 %copy-start = (bf16[16,64,1024]{2,1,0:T(8,128)(2,1)S(1)}, bf16[16,64,1024]{2,1,0:T(8,128)(2,1)}, u32[]{:S(2)}) copy-start(bf16[16,64,1024]{2,1,0:T(8,128)(2,1)} %records.3) | copy-start | bytes 6291460
  1.6 0.7 %copy-start.4 = (s32[16,64]{1,0:T(8,128)S(1)}, s32[16,64]{1,0:T(8,128)}, u32[]{:S(2)}) copy-start(s32[16,64]{1,0:T(8,128)} %valid.3) | copy-start | bytes 12292
  2.3 0.7 %copy-start.5 = (s32[8]{0:T(128)S(1)}, s32[8]{0:T(128)}, u32[]{:S(2)}) copy-start(s32[8]{0:T(128)} %sources.1) | copy-start | bytes 100
  2.9 5.4 %copy-start.1 = (bf16[16,64,1024]{2,1,0:T(8,128)(2,1)S(1)}, bf16[16,64,1024]{2,1,0:T(8,128)(2,1)}, u32[]{:S(2)}) copy-start(bf16[16,64,1024]{2,1,0:T(8,128)(2,1)} %records.3) | copy-start | bytes 6291460
  3.7 11.2 %collective-permute-start = (bf16[8,16,1024]{2,1,0:T(8,128)(2,1)S(1)}, bf16[8,16,1024]{2,1,0:T(8,128)(2,1)S(1)}, u32[]{:S(2)}, u32[]{:S(2)}) collective-permute-start(bf16[8,16,1024]{2,1,0:T(8,128)(2,1)S(1)} %get-tuple-element.13), channel_id=1, source_target_pairs={{0,6},{2,4},{4,2},{6,0},{8,14},{10,12},{12,10},{14,8},{1,7},{3,5},... | collective-permute-start | bytes 786440 | tf_op jit(solution)/shard_map/ppermute | solution.py:230
  7.7 11.9 %collective-permute-start.1 = (bf16[8,16,1024]{2,1,0:T(8,128)(2,1)S(1)}, bf16[8,16,1024]{2,1,0:T(8,128)(2,1)S(1)}, u32[]{:S(2)}, u32[]{:S(2)}) collective-permute-start(bf16[8,16,1024]{2,1,0:T(8,128)(2,1)S(1)} %get-tuple-element.14), channel_id=1, source_target_pairs={{0,2},{2,0},{4,6},{6,4},{8,10},{10,8},{12,14},{14,12},{1,3},{3,1},... | collective-permute-start | bytes 786440 | tf_op jit(solution)/shard_map/ppermute | solution.py:230
  8.3 11.6 %collective-permute-start.2 = (bf16[8,16,1024]{2,1,0:T(8,128)(2,1)S(1)}, bf16[8,16,1024]{2,1,0:T(8,128)(2,1)S(1)}, u32[]{:S(2)}, u32[]{:S(2)}) collective-permute-start(bf16[8,16,1024]{2,1,0:T(8,128)(2,1)S(1)} %get-tuple-element.15), channel_id=1, source_target_pairs={{0,4},{2,6},{4,0},{6,2},{8,12},{10,14},{12,8},{14,10},{1,5},{3,7},... | collective-permute-start | bytes 786440 | tf_op jit(solution)/shard_map/ppermute | solution.py:230
  8.3 1.6 %copy-start.2 = (bf16[1024,1024]{1,0:T(8,128)(2,1)S(1)}, bf16[1024,1024]{1,0:T(8,128)(2,1)}, u32[]{:S(2)}) copy-start(bf16[1024,1024]{1,0:T(8,128)(2,1)} %constant.5.clone.table) | copy-start | bytes 6291460
  9.9 24.8 %copy-start.3 = (bf16[1024,1024]{1,0:T(8,128)(2,1)S(1)}, bf16[1024,1024]{1,0:T(8,128)(2,1)}, u32[]{:S(2)}) copy-start(bf16[1024,1024]{1,0:T(8,128)(2,1)} %constant.5.clone.table) | copy-start | bytes 6291460
  20.0 14.8 %collective-permute-start.3 = (bf16[8,16,1024]{2,1,0:T(8,128)(2,1)S(1)}, bf16[8,16,1024]{2,1,0:T(8,128)(2,1)S(1)}, u32[]{:S(2)}, u32[]{:S(2)}) collective-permute-start(bf16[8,16,1024]{2,1,0:T(8,128)(2,1)S(1)} %add_add_fusion.mine), channel_id=1, source_target_pairs={{0,8},{2,10},{4,12},{6,14},{8,0},{10,2},{12,4},{14,6},{1,9},{3,11}... | collective-permute-start | bytes 786440 | tf_op jit(solution)/shard_map/ppermute | solution.py:230
  35.4 8.2 %collective-permute-start.6 = (bf16[128,1024]{1,0:T(8,128)(2,1)S(1)}, bf16[128,1024]{1,0:T(8,128)(2,1)S(1)}, u32[]{:S(2)}, u32[]{:S(2)}) collective-permute-start(bf16[128,1024]{1,0:T(8,128)(2,1)S(1)} %whiten.1.white), channel_id=1, source_target_pairs={{0,2},{2,0},{4,6},{6,4},{8,10},{10,8},{12,14},{14,12},{1,3},{3,1},... | collective-permute-start | bytes 786440 | tf_op jit(solution)/shard_map/ppermute | solution.py:230
  36.6 9.2 %collective-permute-start.5 = (bf16[128,1024]{1,0:T(8,128)(2,1)S(1)}, bf16[128,1024]{1,0:T(8,128)(2,1)S(1)}, u32[]{:S(2)}, u32[]{:S(2)}) collective-permute-start(bf16[128,1024]{1,0:T(8,128)(2,1)S(1)} %whiten.1.white), channel_id=1, source_target_pairs={{0,4},{2,6},{4,0},{6,2},{8,12},{10,14},{12,8},{14,10},{1,5},{3,7},... | collective-permute-start | bytes 786440 | tf_op jit(solution)/shard_map/ppermute | solution.py:230
  36.6 13.4 %collective-permute-start.4 = (bf16[128,1024]{1,0:T(8,128)(2,1)S(1)}, bf16[128,1024]{1,0:T(8,128)(2,1)S(1)}, u32[]{:S(2)}, u32[]{:S(2)}) collective-permute-start(bf16[128,1024]{1,0:T(8,128)(2,1)S(1)} %whiten.1.white), channel_id=1, source_target_pairs={{0,6},{2,4},{4,2},{6,0},{8,14},{10,12},{12,10},{14,8},{1,7},{3,5},... | collective-permute-start | bytes 786440 | tf_op jit(solution)/shard_map/ppermute | solution.py:230
  50.8 1.6 %collective-permute-start.7 = (f32[16,8,512]{2,1,0:T(8,128)S(1)}, f32[16,8,512]{2,1,0:T(8,128)S(1)}, u32[]{:S(2)}, u32[]{:S(2)}) collective-permute-start(f32[16,8,512]{2,1,0:T(8,128)S(1)} %cross_send.1), channel_id=1, source_target_pairs={{0,1},{1,0},{2,3},{3,2},{4,5},{5,4},{6,7},{7,6},{8,9},{9,8},{10,11... | collective-permute-start | bytes 786440 | tf_op jit(solution)/shard_map/ppermute | solution.py:249
